TPU v7x, 32 devices: a whole 2x2x4 slice. The times are simulated.
32 devices in a mesh: tile: 8 (over y, x, core), trac: 4 (over z).
Axes of the slice: x: 2, y: 2, z: 4, core: 2. Of those that a mesh axis runs over, the one named last changes fastest.
Arguments:
- tracers: float32 [128, 512, 128], P(None, ('tile', 'trac')), may hold values from -6 to 6
- winds: float32 [2, 512, 128], P(None, ('tile', 'trac')), may hold values from -4 to 4
- chem_linear: float32 [128, 128], replicated, may hold values from -0.5 to 0.5
- chem_loss: float32 [128], replicated, may hold values from 0.5 to 4
- chem_left: float32 [4, 128, 128], replicated, may hold values from -0.25 to 0.25
- chem_right: float32 [4, 128, 128], replicated, may hold values from -0.25 to 0.25
- active_cells: int32 [32], P(('tile', 'trac')), may hold values from 256 to 2048
Outputs:
- tracers_out: float32 [128, 512, 128], P(None, ('tile', 'trac'))
- winds_out: float32 [2, 512, 128], P(None, ('tile', 'trac'))
Inputs may be any that keep to these rules, and one draw needn't show every extreme that they name: `active_cells`: active cells are the leading ones of the tile in row-major order.
All inputs are finite; a program needn't handle non-finite values.
Results may differ from a plain program's by a relative error of at most 0.0003.
Values sent between devices are 32-bit elements; how exact they have to be, the bound alone decides.
A program may use at most 64 MiB of HBM per device.

v0:
```python
import functools

import jax
import jax.numpy as jnp
from jax import lax
from jax.experimental import pallas as pl
from jax.experimental.pallas import tpu as pltpu
from jax.sharding import PartitionSpec as P

SUBS = 4
CHEM_STEPS = 3
WIND_STAGES = 3
PARTS = 4
LEAD = 2

DT_WIND = 0.1
VISCOSITY = 0.2
DT_TRACER = 0.1
DT_CHEM = 0.1

AXES = ("tile", "trac")
MESH = pl.DeviceIdType.MESH


def kernel(
    sizes,
    active,
    tracers,
    winds,
    linear,
    loss,
    left,
    right,
    done,
    wind_new,
    lev,
    wind,
    coef,
    lin_v,
    loss_v,
    fac_v,
    weights,
    row_sem,
    par_sem,
    wind_sem,
    send_sem,
    recv_sem,
    wsend_sem,
    wrecv_sem,
    count_ref,
    count_sem,
):
    tiles, tracs = sizes
    species, rows, width = tracers.shape
    pairs = left.shape[0]
    depth = SUBS
    reach = SUBS + WIND_STAGES
    wrows = wind.shape[1]
    base = (wrows - rows) // 2
    shift = base - depth
    devices = tiles * tracs
    me = lax.axis_index(AXES[0]) * tracs + lax.axis_index(AXES[1])
    up_flat = lax.rem(me + 1, devices)
    down_flat = lax.rem(me + devices - 1, devices)
    up = (up_flat // tracs, lax.rem(up_flat, tracs))
    down = (down_flat // tracs, lax.rem(down_flat, tracs))

    barrier = pltpu.get_barrier_semaphore()
    for neighbour in (up, down):
        pl.semaphore_signal(barrier, inc=1, device_id=neighbour, device_id_type=MESH)

    order = []
    for k in range(depth):
        order += [rows - 1 - k, k]
    order += list(range(depth, rows - depth))

    def row_copy(r):
        return pltpu.make_async_copy(tracers.at[:, r, :], lev.at[0, depth + r], row_sem.at[r])

    own_wind = pltpu.make_async_copy(winds, wind.at[:, base : base + rows, :], wind_sem)
    own_wind.start()
    for r in order:
        row_copy(r).start()
    params = [
        pltpu.make_async_copy(linear, lin_v, par_sem.at[0]),
        pltpu.make_async_copy(loss, loss_v, par_sem.at[1]),
        pltpu.make_async_copy(left, fac_v.at[0], par_sem.at[2]),
        pltpu.make_async_copy(right, fac_v.at[1], par_sem.at[3]),
    ]
    for copy in params:
        copy.start()
    count_copy = pltpu.make_async_copy(active, count_ref, count_sem)
    count_copy.start()

    def wind_send(side):
        first = rows - reach if side == 0 else 0
        there = base - reach if side == 0 else base + rows
        return pltpu.make_async_remote_copy(
            src_ref=winds.at[:, first : first + reach, :],
            dst_ref=wind.at[:, there : there + reach, :],
            send_sem=wsend_sem.at[side],
            recv_sem=wrecv_sem.at[side],
            device_id=up if side == 0 else down,
            device_id_type=MESH,
        )

    def halo_send(side, k):
        here = rows - 1 - k if side == 0 else k
        there = depth - 1 - k if side == 0 else depth + rows + k
        return pltpu.make_async_remote_copy(
            src_ref=tracers.at[:, here, :],
            dst_ref=lev.at[0, there],
            send_sem=send_sem.at[side, k],
            recv_sem=recv_sem.at[side, k],
            device_id=up if side == 0 else down,
            device_id_type=MESH,
        )

    pl.semaphore_wait(barrier, 2)
    place = lax.axis_index(AXES[1])
    last = tracs - 1

    @pl.when(jnp.logical_and(place > 0, place < last))
    def _():
        for side in range(2):
            wind_send(side).start()
        for k in range(depth):
            for side in range(2):
                halo_send(side, k).start()

    for end, near in ((0, 0), (last, 1)):

        @pl.when(place == end)
        def _(near=near):
            wind_send(1 - near).start()
            wind_send(near).start()
            for k in range(depth + LEAD):
                if k < depth:
                    halo_send(1 - near, k).start()
                if k >= LEAD:
                    halo_send(near, k - LEAD).start()

    for copy in params:
        copy.wait()
    diag = lax.broadcasted_iota(jnp.int32, (species, species), 0) == lax.broadcasted_iota(
        jnp.int32, (species, species), 1
    )

    block = species // PARTS
    height = (1 + 2 * pairs) * block

    def put(slot, value):
        high = value.astype(jnp.bfloat16)
        low = (value - high.astype(jnp.float32)).astype(jnp.bfloat16)
        for part in range(PARTS):
            lines = pl.ds((part * (1 + 2 * pairs) + slot) * block, block)
            own = slice(part * block, (part + 1) * block)
            weights[lines, :species] = high[own]
            weights[lines, species : 2 * species] = low[own]

    put(0, DT_CHEM * (lin_v[...] - jnp.where(diag, loss_v[...], 0.0)))
    for p in range(pairs):
        put(1 + p, DT_CHEM * fac_v[0, p])
        put(1 + pairs + p, fac_v[1, p])

    for r in range(rows):
        row_copy(r).wait()
    own_wind.wait()

    def update_winds(lines):
        raw = wind[:, lines]
        u0, v0 = raw[0], raw[1]
        held = u0.shape[0]

        def tendency(u, v):
            def of(f):
                east = pltpu.roll(f, width - 1, 1)
                west = pltpu.roll(f, 1, 1)
                north = pltpu.roll(f, held - 1, 0)
                south = pltpu.roll(f, 1, 0)
                along = (east - west) * 0.5
                across = (north - south) * 0.5
                spread = east + west + north + south - 4.0 * f
                return -(u * along + v * across) + VISCOSITY * spread

            return of(u), of(v)

        tu, tv = tendency(u0, v0)
        u1, v1 = u0 + DT_WIND * tu, v0 + DT_WIND * tv
        tu, tv = tendency(u1, v1)
        u2 = 0.75 * u0 + 0.25 * (u1 + DT_WIND * tu)
        v2 = 0.75 * v0 + 0.25 * (v1 + DT_WIND * tv)
        tu, tv = tendency(u2, v2)
        u3 = u0 / 3.0 + 2.0 / 3.0 * (u2 + DT_WIND * tu)
        v3 = v0 / 3.0 + 2.0 / 3.0 * (v2 + DT_WIND * tv)
        if held == wrows:
            wind_new[0] = u3[base : base + rows]
            wind_new[1] = v3[base : base + rows]
        coef[0, lines] = 1.0 - DT_TRACER * (jnp.abs(u3) + jnp.abs(v3))
        coef[1, lines] = pltpu.roll(DT_TRACER * jnp.maximum(u3, 0.0), 1, 1)
        coef[2, lines] = pltpu.roll(-DT_TRACER * jnp.minimum(u3, 0.0), width - 1, 1)
        coef[3, lines] = pltpu.roll(DT_TRACER * jnp.maximum(v3, 0.0), 1, 0)
        coef[4, lines] = pltpu.roll(-DT_TRACER * jnp.minimum(v3, 0.0), held - 1, 0)

    def line(i):
        return pl.ds(i + shift, 1)

    def spread(level, i):
        q = lev[level - 1, i]
        moved = coef[0, line(i), :] * q
        moved += coef[1, line(i), :] * pltpu.roll(q, 1, 1)
        moved += coef[2, line(i), :] * pltpu.roll(q, width - 1, 1)
        return moved

    def advance(level, i):
        moved = spread(level, i)
        moved += coef[3, line(i), :] * lev[level - 1, i - 1]
        moved += coef[4, line(i), :] * lev[level - 1, i + 1]
        lev[level, i] = moved

    def sweep(spans):
        for level, first, last in spans:
            for i in range(first, last):
                advance(level, i)
                yield

    count_copy.wait()
    count = count_ref[0]
    lane = lax.broadcasted_iota(jnp.int32, (1, width), 1)

    def react(couples, values=None):
        concs, masks = [], []
        for n, (first, second) in enumerate(couples):
            pair = (lev[depth, first], lev[depth, second]) if values is None else values[n]
            concs.append(jnp.concatenate(pair, axis=1))
            cell = jnp.concatenate(
                [(first - depth) * width + lane, (second - depth) * width + lane], axis=1
            )
            masks.append(jnp.where(cell < count, 1.0, 0.0))
        for step in range(CHEM_STEPS):
            for j, mask in enumerate(masks):
                conc = concs[j]
                high = conc.astype(jnp.bfloat16)
                low = (conc - high.astype(jnp.float32)).astype(jnp.bfloat16)
                high = jnp.concatenate([high, high], axis=0)
                low = jnp.concatenate([low, low], axis=0)
                blocks = []
                for part in range(PARTS):
                    lhs = weights[part * height : (part + 1) * height]
                    terms = jnp.dot(lhs, high, preferred_element_type=jnp.float32) + jnp.dot(
                        lhs, low, preferred_element_type=jnp.float32
                    )
                    rate = terms[:block]
                    for p in range(pairs):
                        one = (1 + p) * block
                        two = (1 + pairs + p) * block
                        rate += terms[one : one + block] * terms[two : two + block]
                    blocks.append(conc[part * block : (part + 1) * block] + rate * mask)
                    yield
                concs[j] = jnp.concatenate(blocks, axis=0)
        for (first, second), conc in zip(couples, concs):
            done[first - depth] = conc[:, :width]
            done[second - depth] = conc[:, width:]

    def weave(main, side=(), pace=1):
        side = iter(side)
        for _ in main:
            for _ in range(pace):
                next(side, None)
        for _ in side:
            pass

    update_winds(slice(base, base + rows))
    low, high = depth, depth + rows
    levels = range(1, depth + 1)
    inner = [(n, low + WIND_STAGES + n, high - WIND_STAGES - n) for n in levels]
    rims = []
    for n in levels:
        rims += [(n, low + n, low + WIND_STAGES + n), (n, high - WIND_STAGES - n, high - n)]
    weave(sweep(inner))

    for side in range(2):
        wind_send(side).wait()
    update_winds(slice(0, wrows))

    def ready(k):
        for n in levels:
            for i, near in ((low - 1 - k + n, 1), (high + k - n, -1)):
                lev[n, i] = spread(n, i) + coef[3 if near < 0 else 4, line(i), :] * lev[n - 1, i + near]
                yield

    def arrive(k):
        for side in range(2):
            halo_send(side, k).wait()
        south, north = lev[0, low - 1 - k], lev[0, high + k]
        for n in levels:
            i, j = low - 1 - k + n, high + k - n
            south = lev[n, i] + coef[3, line(i), :] * south
            north = lev[n, j] + coef[4, line(j), :] * north
            lev[n, i] = south
            lev[n, j] = north
        return south, north

    couples = [(low + depth + i, high - depth - 1 - i) for i in reversed(range(-depth, WIND_STAGES + 1))]
    first = couples[:1]
    assert 2 * WIND_STAGES + 2 == rows - 2 * depth
    weave(react(first), sweep(rims), -(-2 * WIND_STAGES * depth // (PARTS * CHEM_STEPS)))
    inside = couples[1 : 1 + WIND_STAGES]
    weave(react(inside), ready(0))
    for k in range(depth):
        values = arrive(k)
        weave(react([couples[1 + WIND_STAGES + k]], [values]), ready(k + 1) if k + 1 < depth else (), -(-2 * depth // (PARTS * CHEM_STEPS)))


def finish(done, wind_new, tracers_out, winds_out, out_sem, wind_sem):
    copies = [pltpu.make_async_copy(wind_new, winds_out, wind_sem)]
    for r in range(done.shape[0]):
        copies.append(pltpu.make_async_copy(done.at[r], tracers_out.at[:, r, :], out_sem.at[r]))
    for copy in copies:
        copy.start()
    for copy in copies:
        copy.wait()


def on_device(sizes, tracers, winds, linear, loss, left, right, active):
    species, rows, width = tracers.shape
    pairs = left.shape[0]
    held = rows + 2 * SUBS
    wrows = rows + 2 * (-(-(SUBS + WIND_STAGES) // 8) * 8)
    f32 = jnp.float32
    dma = pltpu.SemaphoreType.DMA
    anywhere = pl.BlockSpec(memory_space=pl.ANY)
    vmem = pl.BlockSpec(memory_space=pltpu.VMEM)
    done, wind_new = pl.pallas_call(
        functools.partial(kernel, sizes),
        out_shape=(
            pltpu.VMEM((rows, species, width), f32),
            pltpu.VMEM(winds.shape, f32),
        ),
        in_specs=[anywhere] * 7,
        out_specs=(vmem, vmem),
        scratch_shapes=[
            pltpu.VMEM((SUBS + 1, held, species, width), f32),
            pltpu.VMEM((2, wrows, width), f32),
            pltpu.VMEM((5, wrows, width), f32),
            pltpu.VMEM(linear.shape, f32),
            pltpu.VMEM((1, species), f32),
            pltpu.VMEM((2,) + left.shape, f32),
            pltpu.VMEM(((1 + 2 * pairs) * species, 2 * species), jnp.bfloat16),
            dma((rows,)),
            dma((4,)),
            dma,
            dma((2, SUBS)),
            dma((2, SUBS)),
            dma((2,)),
            dma((2,)),
            pltpu.SMEM(active.shape, active.dtype),
            dma,
        ],
        compiler_params=pltpu.CompilerParams(collective_id=0, has_side_effects=True),
    )(active, tracers, winds, linear, loss.reshape(1, species), left, right)
    return pl.pallas_call(
        finish,
        out_shape=(
            jax.ShapeDtypeStruct(tracers.shape, f32),
            jax.ShapeDtypeStruct(winds.shape, f32),
        ),
        in_specs=[vmem, vmem],
        out_specs=(anywhere, anywhere),
        scratch_shapes=[dma((rows,)), dma],
    )(
        pltpu.with_memory_space_constraint(done, pltpu.VMEM),
        pltpu.with_memory_space_constraint(wind_new, pltpu.VMEM),
    )


def solution(mesh):
    sizes = tuple(mesh.shape[axis] for axis in AXES)
    banded = P(None, AXES, None)
    return jax.shard_map(
        functools.partial(on_device, sizes),
        mesh=mesh,
        in_specs=(banded, banded, P(), P(), P(), P(), P(AXES)),
        out_specs=(banded, banded),
        check_vma=False,
    )
```

profile of v0, /device:TPU:0, one launch (start us, length us, event | category | flops | bytes accessed | tf_op | source)
XLA Modules:
  0.0 23.3 jit_solution(8078416265715457837)
XLA Ops:
  1.3 20.9 %shard_map.86 = (f32[16,128,128]{2,1,0:T(8,128)S(1)}, f32[2,16,128]{2,1,0:T(8,128)S(1)}) custom-call(s32[1]{0:T(128)S(6)} %copy.9.active, f32[128,16,128]{2,1,0:T(8,128)} %tracers.1, f32[2,16,128]{2,1,0:T(8,128)} %winds.1, f32[128,128]{1,0:T(8,128)} %linear.1, f32[1,128]{1,0:T(1,128)} %bitcast.1, f32[4,128,128]{2,1,0:T(8,128)} %left.1, f32[4,128,128]{2,1,0:T(8,128)} %right.1), custom_call_target="tpu_custom_call" | custom-call | tf_op jit(solution)/shard_map/pallas_call | solution.py:334
  22.2 1.1 %shard_map.87 = (f32[128,16,128]{2,1,0:T(8,128)}, f32[2,16,128]{2,1,0:T(8,128)}) custom-call(f32[16,128,128]{2,1,0:T(8,128)S(1)} %get-tuple-element.4.done, f32[2,16,128]{2,1,0:T(8,128)S(1)} %get-tuple-element.5.wind_new), custom_call_target="tpu_custom_call" | custom-call | tf_op jit(solution)/shard_map/pallas_call | solution.py:362
where the time goes:
time: 23.5 us; the launch traced here: 23.3 us
  Pallas kernels  22 us (94%)
  between operations  1.29 us (5%)
    pallas_call x1, Pallas kernels, on_device(): pl.pallas_call(functools.partial(kernel, sizes), out_shape=(pltpu.VMEM((r...  20.9 us
    pallas_call x1, Pallas kernels, on_device(): pl.pallas_call(finish, out_shape=(jax.ShapeDtypeStruct(tracers.shape, f32...  1.11 us

commit v1 on v0

--- a/solution.py
+++ b/solution.py
@@ -10,8 +10,11 @@
 SUBS = 4
 CHEM_STEPS = 3
 WIND_STAGES = 3
-PARTS = 4
-LEAD = 2
+PARTS = 8
+LEAD = (1, 1)
+EARLY = 2
+MIDDLE = 4
+LATE = 1
 
 DT_WIND = 0.1
 VISCOSITY = 0.2
@@ -49,6 +52,7 @@
     wrecv_sem,
     count_ref,
     count_sem,
+    joined,
 ):
     tiles, tracs = sizes
     species, rows, width = tracers.shape
@@ -65,9 +69,22 @@
     up = (up_flat // tracs, lax.rem(up_flat, tracs))
     down = (down_flat // tracs, lax.rem(down_flat, tracs))
 
+    place = lax.axis_index(AXES[1])
+    last = tracs - 1
+
+    def tell(semaphore, neighbour):
+        pl.semaphore_signal(semaphore, inc=1, device_id=neighbour, device_id_type=MESH)
+
     barrier = pltpu.get_barrier_semaphore()
-    for neighbour in (up, down):
-        pl.semaphore_signal(barrier, inc=1, device_id=neighbour, device_id_type=MESH)
+
+    @pl.when(place < last)
+    def _():
+        tell(barrier, up)
+
+    @pl.when(place < 2)
+    def _():
+        tell(barrier, down)
+
 
     order = []
     for k in range(depth):
@@ -116,29 +133,54 @@
             device_id_type=MESH,
         )
 
-    pl.semaphore_wait(barrier, 2)
-    place = lax.axis_index(AXES[1])
-    last = tracs - 1
+    pl.semaphore_wait(barrier, jnp.where(place == last, 2, 1))
+
+    @pl.when(place > 1)
+    def _():
+        tell(joined, down)
+
+    @pl.when(place == last)
+    def _():
+        tell(joined, up)
+
+    def send(side):
+        wind_send(side).start()
+        for k in range(MIDDLE):
+            halo_send(side, k).start()
+
+    def late(at):
+        if at != LATE:
+            return
+
+        @pl.when(jnp.logical_and(place > 0, place < last))
+        def _():
+            for k in range(MIDDLE, depth):
+                for side in range(2):
+                    halo_send(side, k).start()
+
+    def both(near, lead, early):
+        turns = [(2 * k + 1, near, k) for k in range(early, depth)]
+        turns += [(2 * (k - lead), 1 - near, k) for k in range(depth)]
+        for _, side, k in sorted(turns):
+            halo_send(side, k).start()
+
+    @pl.when(place == 0)
+    def _():
+        wind_send(0).start()
+        for k in range(EARLY):
+            halo_send(0, k).start()
 
     @pl.when(jnp.logical_and(place > 0, place < last))
     def _():
-        for side in range(2):
-            wind_send(side).start()
-        for k in range(depth):
-            for side in range(2):
-                halo_send(side, k).start()
-
-    for end, near in ((0, 0), (last, 1)):
-
-        @pl.when(place == end)
-        def _(near=near):
-            wind_send(1 - near).start()
-            wind_send(near).start()
-            for k in range(depth + LEAD):
-                if k < depth:
-                    halo_send(1 - near, k).start()
-                if k >= LEAD:
-                    halo_send(near, k - LEAD).start()
+        send(1)
+        pl.semaphore_wait(joined, 1)
+        send(0)
+
+    @pl.when(place == last)
+    def _():
+        wind_send(0).start()
+        wind_send(1).start()
+        both(1, LEAD[1], 0)
 
     for copy in params:
         copy.wait()
@@ -274,13 +316,19 @@
     low, high = depth, depth + rows
     levels = range(1, depth + 1)
     inner = [(n, low + WIND_STAGES + n, high - WIND_STAGES - n) for n in levels]
-    rims = []
-    for n in levels:
-        rims += [(n, low + n, low + WIND_STAGES + n), (n, high - WIND_STAGES - n, high - n)]
+    couples = [(low + depth + i, high - depth - 1 - i) for i in reversed(range(-depth, WIND_STAGES + 1))]
+    assert 2 * WIND_STAGES + 2 == rows - 2 * depth
     weave(sweep(inner))
 
+    @pl.when(place == 0)
+    def _():
+        pl.semaphore_wait(joined, 1)
+        wind_send(1).start()
+        both(0, LEAD[0], EARLY)
+
+    weave(react(couples[:1]))
     for side in range(2):
-        wind_send(side).wait()
+        wind_send(side).wait_recv()
     update_winds(slice(0, wrows))
 
     def ready(k):
@@ -291,7 +339,7 @@
 
     def arrive(k):
         for side in range(2):
-            halo_send(side, k).wait()
+            halo_send(side, k).wait_recv()
         south, north = lev[0, low - 1 - k], lev[0, high + k]
         for n in levels:
             i, j = low - 1 - k + n, high + k - n
@@ -301,15 +349,29 @@
             lev[n, j] = north
         return south, north
 
-    couples = [(low + depth + i, high - depth - 1 - i) for i in reversed(range(-depth, WIND_STAGES + 1))]
-    first = couples[:1]
-    assert 2 * WIND_STAGES + 2 == rows - 2 * depth
-    weave(react(first), sweep(rims), -(-2 * WIND_STAGES * depth // (PARTS * CHEM_STEPS)))
-    inside = couples[1 : 1 + WIND_STAGES]
-    weave(react(inside), ready(0))
+    def rim(d):
+        for n in levels:
+            for i in (low + WIND_STAGES + n - 1 - d, high - WIND_STAGES - n + d):
+                advance(n, i)
+                yield
+
+    def chain(*parts):
+        for part in parts:
+            yield from part
+
+    late(0)
+    weave(rim(0))
+    weave(react(couples[1:2]), chain(rim(1), rim(2)), 2)
+    late(1)
+    weave(react(couples[2 : 1 + WIND_STAGES]), ready(0))
+    late(2)
     for k in range(depth):
         values = arrive(k)
         weave(react([couples[1 + WIND_STAGES + k]], [values]), ready(k + 1) if k + 1 < depth else (), -(-2 * depth // (PARTS * CHEM_STEPS)))
+    for side in range(2):
+        wind_send(side).wait_send()
+        for k in range(depth):
+            halo_send(side, k).wait_send()
 
 
 def finish(done, wind_new, tracers_out, winds_out, out_sem, wind_sem):
@@ -356,6 +418,7 @@
             dma((2,)),
             pltpu.SMEM(active.shape, active.dtype),
             dma,
+            pltpu.SemaphoreType.REGULAR,
         ],
         compiler_params=pltpu.CompilerParams(collective_id=0, has_side_effects=True),
     )(active, tracers, winds, linear, loss.reshape(1, species), left, right)

time: 23.5 us -> 21.3 us (0.906)
  Pallas kernels: 22 us -> 19.6 us
    pallas_call x1, Pallas kernels: 20.9 us -> 18.5 us  [on_device(): pl.pallas_call(functools.partial(kernel, sizes), out_shape=(pltpu.VMEM((r...]
where the time goes in v1:
time: 21.3 us; the launch traced here: 20.9 us
  Pallas kernels  19.6 us (92%)
  between operations  1.29 us (6%)
    pallas_call x1, Pallas kernels, on_device(): pl.pallas_call(functools.partial(kernel, sizes), out_shape=(pltpu.VMEM((r...  18.5 us
    pallas_call x1, Pallas kernels, on_device(): pl.pallas_call(finish, out_shape=(jax.ShapeDtypeStruct(tracers.shape, f32...  1.11 us

profile of v1, /device:TPU:0, one launch (start us, length us, event | category | flops | bytes accessed | tf_op | source)
XLA Modules:
  0.0 20.9 jit_solution(10910189923732559323)
XLA Ops:
  1.3 18.5 %shard_map.86 = (f32[16,128,128]{2,1,0:T(8,128)S(1)}, f32[2,16,128]{2,1,0:T(8,128)S(1)}) custom-call(s32[1]{0:T(128)S(6)} %copy.9.active, f32[128,16,128]{2,1,0:T(8,128)} %tracers.1, f32[2,16,128]{2,1,0:T(8,128)} %winds.1, f32[128,128]{1,0:T(8,128)} %linear.1, f32[1,128]{1,0:T(1,128)} %bitcast.1, f32[4,128,128]{2,1,0:T(8,128)} %left.1, f32[4,128,128]{2,1,0:T(8,128)} %right.1), custom_call_target="tpu_custom_call" | custom-call | tf_op jit(solution)/shard_map/pallas_call | solution.py:396
  19.8 1.1 %shard_map.87 = (f32[128,16,128]{2,1,0:T(8,128)}, f32[2,16,128]{2,1,0:T(8,128)}) custom-call(f32[16,128,128]{2,1,0:T(8,128)S(1)} %get-tuple-element.4.done, f32[2,16,128]{2,1,0:T(8,128)S(1)} %get-tuple-element.5.wind_new), custom_call_target="tpu_custom_call" | custom-call | tf_op jit(solution)/shard_map/pallas_call | solution.py:425

commit v2 on v1

--- a/solution.py
+++ b/solution.py
@@ -10,11 +10,12 @@
 SUBS = 4
 CHEM_STEPS = 3
 WIND_STAGES = 3
-PARTS = 8
-LEAD = (1, 1)
+PARTS = 4
+PIECES = 2
+LEAD = (2, 2)
 EARLY = 2
 MIDDLE = 4
-LATE = 1
+LATE = 0
 
 DT_WIND = 0.1
 VISCOSITY = 0.2
@@ -23,6 +24,36 @@
 
 AXES = ("tile", "trac")
 MESH = pl.DeviceIdType.MESH
+
+
+def chemistry(weights, concs, masks, store=None):
+    species = concs[0].shape[0]
+    block = species // PARTS
+    height = weights.shape[0] // PARTS
+    pairs = (height // block - 1) // 2
+    for step in range(CHEM_STEPS):
+        for j, mask in enumerate(masks):
+            conc = concs[j]
+            high = conc.astype(jnp.bfloat16)
+            low = (conc - high.astype(jnp.float32)).astype(jnp.bfloat16)
+            high = jnp.concatenate([high, high], axis=0)
+            low = jnp.concatenate([low, low], axis=0)
+            blocks = []
+            for part in range(PARTS):
+                lhs = weights[part * height : (part + 1) * height]
+                terms = jnp.dot(lhs, high, preferred_element_type=jnp.float32) + jnp.dot(
+                    lhs, low, preferred_element_type=jnp.float32
+                )
+                rate = terms[:block]
+                for p in range(pairs):
+                    one = (1 + p) * block
+                    two = (1 + pairs + p) * block
+                    rate += terms[one : one + block] * terms[two : two + block]
+                blocks.append(conc[part * block : (part + 1) * block] + rate * mask)
+                if store is not None and step == CHEM_STEPS - 1:
+                    store(part, blocks[-1])
+                yield
+            concs[j] = jnp.concatenate(blocks, axis=0)
 
 
 def kernel(
@@ -36,13 +67,14 @@
     right,
     done,
     wind_new,
+    weights,
+    mask_out,
     lev,
     wind,
     coef,
     lin_v,
     loss_v,
     fac_v,
-    weights,
     row_sem,
     par_sem,
     wind_sem,
@@ -270,36 +302,17 @@
     count = count_ref[0]
     lane = lax.broadcasted_iota(jnp.int32, (1, width), 1)
 
+    def mask_of(*pair):
+        cell = jnp.concatenate([(i - depth) * width + lane for i in pair], axis=1)
+        return jnp.where(cell < count, 1.0, 0.0)
+
     def react(couples, values=None):
         concs, masks = [], []
         for n, (first, second) in enumerate(couples):
             pair = (lev[depth, first], lev[depth, second]) if values is None else values[n]
             concs.append(jnp.concatenate(pair, axis=1))
-            cell = jnp.concatenate(
-                [(first - depth) * width + lane, (second - depth) * width + lane], axis=1
-            )
-            masks.append(jnp.where(cell < count, 1.0, 0.0))
-        for step in range(CHEM_STEPS):
-            for j, mask in enumerate(masks):
-                conc = concs[j]
-                high = conc.astype(jnp.bfloat16)
-                low = (conc - high.astype(jnp.float32)).astype(jnp.bfloat16)
-                high = jnp.concatenate([high, high], axis=0)
-                low = jnp.concatenate([low, low], axis=0)
-                blocks = []
-                for part in range(PARTS):
-                    lhs = weights[part * height : (part + 1) * height]
-                    terms = jnp.dot(lhs, high, preferred_element_type=jnp.float32) + jnp.dot(
-                        lhs, low, preferred_element_type=jnp.float32
-                    )
-                    rate = terms[:block]
-                    for p in range(pairs):
-                        one = (1 + p) * block
-                        two = (1 + pairs + p) * block
-                        rate += terms[one : one + block] * terms[two : two + block]
-                    blocks.append(conc[part * block : (part + 1) * block] + rate * mask)
-                    yield
-                concs[j] = jnp.concatenate(blocks, axis=0)
+            masks.append(mask_of(first, second))
+        yield from chemistry(weights, concs, masks)
         for (first, second), conc in zip(couples, concs):
             done[first - depth] = conc[:, :width]
             done[second - depth] = conc[:, width:]
@@ -365,21 +378,44 @@
     late(1)
     weave(react(couples[2 : 1 + WIND_STAGES]), ready(0))
     late(2)
-    for k in range(depth):
+    for k in range(depth - 1):
         values = arrive(k)
-        weave(react([couples[1 + WIND_STAGES + k]], [values]), ready(k + 1) if k + 1 < depth else (), -(-2 * depth // (PARTS * CHEM_STEPS)))
+        pace = -(-2 * depth // (PARTS * CHEM_STEPS))
+        weave(react([couples[1 + WIND_STAGES + k]], [values]), ready(k + 1), pace)
+    mask_out[...] = mask_of(low, high - 1)
+    done[0], done[rows - 1] = arrive(depth - 1)
     for side in range(2):
         wind_send(side).wait_send()
         for k in range(depth):
             halo_send(side, k).wait_send()
 
 
-def finish(done, wind_new, tracers_out, winds_out, out_sem, wind_sem):
+def finish(done, wind_new, weights, mask, tracers_out, winds_out, tail, out_sem, tail_sem, wind_sem):
+    rows, species, width = done.shape
+    block = species // PARTS
     copies = [pltpu.make_async_copy(wind_new, winds_out, wind_sem)]
-    for r in range(done.shape[0]):
+    for r in range(1, rows - 1):
         copies.append(pltpu.make_async_copy(done.at[r], tracers_out.at[:, r, :], out_sem.at[r]))
     for copy in copies:
         copy.start()
+
+    def store(part, values):
+        own = slice(part * block, (part + 1) * block)
+        tail[0, own] = values[:, :width]
+        tail[1, own] = values[:, width:]
+        if (part + 1) % (PARTS // PIECES) == 0:
+            piece = (part + 1) // (PARTS // PIECES) - 1
+            span = slice(piece * species // PIECES, (piece + 1) * species // PIECES)
+            for end, r in ((0, 0), (1, rows - 1)):
+                copy = pltpu.make_async_copy(
+                    tail.at[end, span], tracers_out.at[span, r, :], tail_sem.at[end, piece]
+                )
+                copy.start()
+                copies.append(copy)
+
+    conc = jnp.concatenate([done[0], done[rows - 1]], axis=1)
+    for _ in chemistry(weights, [conc], [mask[...]], store):
+        pass
     for copy in copies:
         copy.wait()
 
@@ -393,14 +429,17 @@
     dma = pltpu.SemaphoreType.DMA
     anywhere = pl.BlockSpec(memory_space=pl.ANY)
     vmem = pl.BlockSpec(memory_space=pltpu.VMEM)
-    done, wind_new = pl.pallas_call(
+    lines = (1 + 2 * pairs) * species
+    held_over = pl.pallas_call(
         functools.partial(kernel, sizes),
         out_shape=(
             pltpu.VMEM((rows, species, width), f32),
             pltpu.VMEM(winds.shape, f32),
+            pltpu.VMEM((lines, 2 * species), jnp.bfloat16),
+            pltpu.VMEM((1, 2 * width), f32),
         ),
         in_specs=[anywhere] * 7,
-        out_specs=(vmem, vmem),
+        out_specs=(vmem,) * 4,
         scratch_shapes=[
             pltpu.VMEM((SUBS + 1, held, species, width), f32),
             pltpu.VMEM((2, wrows, width), f32),
@@ -408,7 +447,6 @@
             pltpu.VMEM(linear.shape, f32),
             pltpu.VMEM((1, species), f32),
             pltpu.VMEM((2,) + left.shape, f32),
-            pltpu.VMEM(((1 + 2 * pairs) * species, 2 * species), jnp.bfloat16),
             dma((rows,)),
             dma((4,)),
             dma,
@@ -428,13 +466,10 @@
             jax.ShapeDtypeStruct(tracers.shape, f32),
             jax.ShapeDtypeStruct(winds.shape, f32),
         ),
-        in_specs=[vmem, vmem],
+        in_specs=[vmem] * 4,
         out_specs=(anywhere, anywhere),
-        scratch_shapes=[dma((rows,)), dma],
-    )(
-        pltpu.with_memory_space_constraint(done, pltpu.VMEM),
-        pltpu.with_memory_space_constraint(wind_new, pltpu.VMEM),
-    )
+        scratch_shapes=[pltpu.VMEM((2, species, width), f32), dma((rows,)), dma((2, PIECES)), dma],
+    )(*(pltpu.with_memory_space_constraint(x, pltpu.VMEM) for x in held_over))
 
 
 def solution(mesh):

time: 21.3 us -> 21.1 us (level)
    pallas_call x1, Pallas kernels: 18.5 us -> 17.1 us  [on_device(): pl.pallas_call(functools.partial(kernel, sizes), out_shape=(pltpu.VMEM((r...]
    pallas_call x1, Pallas kernels: 1.11 us -> 2.32 us  [on_device(): pl.pallas_call(finish, out_shape=(jax.ShapeDtypeStruct(tracers.shape, f32...]
where the time goes in v2:
time: 21.1 us; the launch traced here: 20.7 us
  Pallas kernels  19.4 us (92%)
  between operations  1.29 us (6%)
    pallas_call x1, Pallas kernels, on_device(): pl.pallas_call(functools.partial(kernel, sizes), out_shape=(pltpu.VMEM((r...  17.1 us
    pallas_call x1, Pallas kernels, on_device(): pl.pallas_call(finish, out_shape=(jax.ShapeDtypeStruct(tracers.shape, f32...  2.32 us

profile of v2, /device:TPU:0, one launch (start us, length us, event | category | flops | bytes accessed | tf_op | source)
XLA Modules:
  0.0 20.7 jit_solution(9791406359097677299)
XLA Ops:
  1.3 17.1 %shard_map.86 = (f32[16,128,128]{2,1,0:T(8,128)S(1)}, f32[2,16,128]{2,1,0:T(8,128)S(1)}, bf16[1152,256]{1,0:T(8,128)(2,1)S(1)}, f32[1,256]{1,0:T(1,128)S(1)}) custom-call(s32[1]{0:T(128)S(6)} %copy.9.active, f32[128,16,128]{2,1,0:T(8,128)} %tracers.1, f32[2,16,128]{2,1,0:T(8,128)} %winds.1, f32[128,128]{1,0:T(8,128)} %linear.1, f32[1,128]{1,0:T(1,128)} %bitcast.1, ...), custom_call_target="tpu_custom_call" | custom-call | tf_op jit(solution)/shard_map/pallas_call | solution.py:433
  18.4 2.3 %shard_map.87 = (f32[128,16,128]{2,1,0:T(8,128)}, f32[2,16,128]{2,1,0:T(8,128)}) custom-call(f32[16,128,128]{2,1,0:T(8,128)S(1)} %get-tuple-element.6.done, f32[2,16,128]{2,1,0:T(8,128)S(1)} %get-tuple-element.7.wind_new, bf16[1152,256]{1,0:T(8,128)(2,1)S(1)} %get-tuple-element.8.weights, f32[1,256]{1,0:T(1,128)S(1)} %get-tuple-element.9.mask), custom_call_target="tpu_custom_call" | custom-call | tf_op jit(solution)/shard_map/pallas_call | solution.py:463

commit v3 on v2

--- a/solution.py
+++ b/solution.py
@@ -10,12 +10,11 @@
 SUBS = 4
 CHEM_STEPS = 3
 WIND_STAGES = 3
-PARTS = 4
+PARTS = 2
 PIECES = 2
-LEAD = (2, 2)
+FLOW = 6
+LEAD = (2, 1)
 EARLY = 2
-MIDDLE = 4
-LATE = 0
 
 DT_WIND = 0.1
 VISCOSITY = 0.2
@@ -177,18 +176,8 @@
 
     def send(side):
         wind_send(side).start()
-        for k in range(MIDDLE):
+        for k in range(depth):
             halo_send(side, k).start()
-
-    def late(at):
-        if at != LATE:
-            return
-
-        @pl.when(jnp.logical_and(place > 0, place < last))
-        def _():
-            for k in range(MIDDLE, depth):
-                for side in range(2):
-                    halo_send(side, k).start()
 
     def both(near, lead, early):
         turns = [(2 * k + 1, near, k) for k in range(early, depth)]
@@ -241,8 +230,8 @@
         row_copy(r).wait()
     own_wind.wait()
 
-    def update_winds(lines):
-        raw = wind[:, lines]
+    def update_winds(first, end, keep_first, keep_end):
+        raw = wind[:, first:end]
         u0, v0 = raw[0], raw[1]
         held = u0.shape[0]
 
@@ -267,14 +256,18 @@
         tu, tv = tendency(u2, v2)
         u3 = u0 / 3.0 + 2.0 / 3.0 * (u2 + DT_WIND * tu)
         v3 = v0 / 3.0 + 2.0 / 3.0 * (v2 + DT_WIND * tv)
-        if held == wrows:
-            wind_new[0] = u3[base : base + rows]
-            wind_new[1] = v3[base : base + rows]
-        coef[0, lines] = 1.0 - DT_TRACER * (jnp.abs(u3) + jnp.abs(v3))
-        coef[1, lines] = pltpu.roll(DT_TRACER * jnp.maximum(u3, 0.0), 1, 1)
-        coef[2, lines] = pltpu.roll(-DT_TRACER * jnp.minimum(u3, 0.0), width - 1, 1)
-        coef[3, lines] = pltpu.roll(DT_TRACER * jnp.maximum(v3, 0.0), 1, 0)
-        coef[4, lines] = pltpu.roll(-DT_TRACER * jnp.minimum(v3, 0.0), held - 1, 0)
+        lines = slice(keep_first, keep_end)
+        own = slice(keep_first - first, keep_end - first)
+        if held > rows:
+            there = slice(max(keep_first, base) - base, min(keep_end, base + rows) - base)
+            here = slice(there.start + base - first, there.stop + base - first)
+            wind_new[0, there] = u3[here]
+            wind_new[1, there] = v3[here]
+        coef[0, lines] = (1.0 - DT_TRACER * (jnp.abs(u3) + jnp.abs(v3)))[own]
+        coef[1, lines] = pltpu.roll(DT_TRACER * jnp.maximum(u3, 0.0), 1, 1)[own]
+        coef[2, lines] = pltpu.roll(-DT_TRACER * jnp.minimum(u3, 0.0), width - 1, 1)[own]
+        coef[3, lines] = pltpu.roll(DT_TRACER * jnp.maximum(v3, 0.0), 1, 0)[own]
+        coef[4, lines] = pltpu.roll(-DT_TRACER * jnp.minimum(v3, 0.0), held - 1, 0)[own]
 
     def line(i):
         return pl.ds(i + shift, 1)
@@ -325,65 +318,98 @@
         for _ in side:
             pass
 
-    update_winds(slice(base, base + rows))
+    update_winds(base, base + rows, base, base + rows)
     low, high = depth, depth + rows
     levels = range(1, depth + 1)
     inner = [(n, low + WIND_STAGES + n, high - WIND_STAGES - n) for n in levels]
     couples = [(low + depth + i, high - depth - 1 - i) for i in reversed(range(-depth, WIND_STAGES + 1))]
-    assert 2 * WIND_STAGES + 2 == rows - 2 * depth
+    assert 2 * WIND_STAGES + 2 == rows - 2 * depth and WIND_STAGES == 3
     weave(sweep(inner))
 
-    @pl.when(place == 0)
-    def _():
+    def answer():
         pl.semaphore_wait(joined, 1)
         wind_send(1).start()
         both(0, LEAD[0], EARLY)
 
+    first_tile = lax.axis_index(AXES[0]) == 0
+    pl.when(jnp.logical_and(place == 0, jnp.logical_not(first_tile)))(answer)
+
     weave(react(couples[:1]))
-    for side in range(2):
-        wind_send(side).wait_recv()
-    update_winds(slice(0, wrows))
-
-    def ready(k):
+    def ready(side, k):
         for n in levels:
-            for i, near in ((low - 1 - k + n, 1), (high + k - n, -1)):
-                lev[n, i] = spread(n, i) + coef[3 if near < 0 else 4, line(i), :] * lev[n - 1, i + near]
-                yield
-
-    def arrive(k):
-        for side in range(2):
+            i, near = (high + k - n, -1) if side else (low - 1 - k + n, 1)
+            lev[n, i] = spread(n, i) + coef[3 if side else 4, line(i), :] * lev[n - 1, i + near]
+            yield
+
+    def arrive(*sides_and_k):
+        *sides, k = sides_and_k
+        for side in sides:
             halo_send(side, k).wait_recv()
-        south, north = lev[0, low - 1 - k], lev[0, high + k]
+        ends = [lev[0, high + k if side else low - 1 - k] for side in sides]
         for n in levels:
-            i, j = low - 1 - k + n, high + k - n
-            south = lev[n, i] + coef[3, line(i), :] * south
-            north = lev[n, j] + coef[4, line(j), :] * north
-            lev[n, i] = south
-            lev[n, j] = north
-        return south, north
-
-    def rim(d):
+            for at, side in enumerate(sides):
+                i = high + k - n if side else low - 1 - k + n
+                ends[at] = lev[n, i] + coef[4 if side else 3, line(i), :] * ends[at]
+                lev[n, i] = ends[at]
+        return ends
+
+    def both_ready(k):
+        return chain(ready(0, k), ready(1, k))
+
+    def rim(side, d):
         for n in levels:
-            for i in (low + WIND_STAGES + n - 1 - d, high - WIND_STAGES - n + d):
-                advance(n, i)
-                yield
+            advance(n, high - WIND_STAGES - n + d if side else low + WIND_STAGES + n - 1 - d)
+            yield
 
     def chain(*parts):
         for part in parts:
             yield from part
 
-    late(0)
-    weave(rim(0))
-    weave(react(couples[1:2]), chain(rim(1), rim(2)), 2)
-    late(1)
-    weave(react(couples[2 : 1 + WIND_STAGES]), ready(0))
-    late(2)
+    halfway = base + rows // 2
+    pace = -(-2 * depth // (PARTS * CHEM_STEPS))
+
+    def one_side(side):
+        wind_send(side).wait_recv()
+        if side:
+            update_winds(base, wrows, halfway, wrows)
+        else:
+            update_winds(0, base + rows, 0, halfway)
+        inner_rows = [couple[side] for couple in couples[1:3]]
+        weave(chain(rim(side, 0), rim(side, 1)))
+        weave(react([inner_rows]), rim(side, 2))
+
+    def rest_inside():
+        weave(react(couples[WIND_STAGES : 1 + WIND_STAGES]), both_ready(0))
+
+    farthest = jnp.logical_and(place == 0, first_tile)
+
+    @pl.when(place == last)
+    def _():
+        one_side(0)
+        one_side(1)
+        rest_inside()
+
+    @pl.when(farthest)
+    def _():
+        one_side(1)
+        answer()
+        one_side(0)
+        rest_inside()
+
+    @pl.when(jnp.logical_and(place < last, jnp.logical_not(farthest)))
+    def _():
+        for side in range(2):
+            wind_send(side).wait_recv()
+        update_winds(0, wrows, 0, wrows)
+        weave(chain(rim(0, 0), rim(1, 0)))
+        weave(react(couples[1:2]), chain(*(rim(side, d) for d in (1, 2) for side in range(2))), 2)
+        weave(react(couples[2 : 1 + WIND_STAGES]), both_ready(0))
+
     for k in range(depth - 1):
-        values = arrive(k)
-        pace = -(-2 * depth // (PARTS * CHEM_STEPS))
-        weave(react([couples[1 + WIND_STAGES + k]], [values]), ready(k + 1), pace)
+        values = arrive(0, 1, k)
+        weave(react([couples[1 + WIND_STAGES + k]], [values]), both_ready(k + 1), pace)
     mask_out[...] = mask_of(low, high - 1)
-    done[0], done[rows - 1] = arrive(depth - 1)
+    done[0], done[rows - 1] = arrive(0, 1, depth - 1)
     for side in range(2):
         wind_send(side).wait_send()
         for k in range(depth):
@@ -396,8 +422,7 @@
     copies = [pltpu.make_async_copy(wind_new, winds_out, wind_sem)]
     for r in range(1, rows - 1):
         copies.append(pltpu.make_async_copy(done.at[r], tracers_out.at[:, r, :], out_sem.at[r]))
-    for copy in copies:
-        copy.start()
+    rest = iter(list(copies))
 
     def store(part, values):
         own = slice(part * block, (part + 1) * block)
@@ -415,7 +440,9 @@
 
     conc = jnp.concatenate([done[0], done[rows - 1]], axis=1)
     for _ in chemistry(weights, [conc], [mask[...]], store):
-        pass
+        for copy in (next(rest, None) for _ in range(FLOW)):
+            if copy is not None:
+                copy.start()
     for copy in copies:
         copy.wait()
 

time: 21.1 us -> 20.7 us (0.981)
  Pallas kernels: 19.4 us -> 18.9 us
    pallas_call x1, Pallas kernels: 17.1 us -> 16.6 us  [on_device(): pl.pallas_call(functools.partial(kernel, sizes), out_shape=(pltpu.VMEM((r...]
where the time goes in v3:
time: 20.7 us; the launch traced here: 20.4 us
  Pallas kernels  18.9 us (91%)
  between operations  1.45 us (7%)
    pallas_call x1, Pallas kernels, on_device(): pl.pallas_call(functools.partial(kernel, sizes), out_shape=(pltpu.VMEM((r...  16.6 us
    pallas_call x1, Pallas kernels, on_device(): pl.pallas_call(finish, out_shape=(jax.ShapeDtypeStruct(tracers.shape, f32...  2.27 us

profile of v3, /device:TPU:0, one launch (start us, length us, event | category | flops | bytes accessed | tf_op | source)
XLA Modules:
  0.0 20.4 jit_solution(4073819270937857391)
XLA Ops:
  1.3 16.6 %shard_map.86 = (f32[16,128,128]{2,1,0:T(8,128)S(1)}, f32[2,16,128]{2,1,0:T(8,128)S(1)}, bf16[1152,256]{1,0:T(8,128)(2,1)S(1)}, f32[1,256]{1,0:T(1,128)S(1)}) custom-call(s32[1]{0:T(128)S(6)} %copy.9.active, f32[128,16,128]{2,1,0:T(8,128)} %tracers.1, f32[2,16,128]{2,1,0:T(8,128)} %winds.1, f32[128,128]{1,0:T(8,128)} %linear.1, f32[1,128]{1,0:T(1,128)} %bitcast.1, ...), custom_call_target="tpu_custom_call" | custom-call | tf_op jit(solution)/shard_map/pallas_call | solution.py:460
  17.9 2.3 %shard_map.87 = (f32[128,16,128]{2,1,0:T(8,128)}, f32[2,16,128]{2,1,0:T(8,128)}) custom-call(f32[16,128,128]{2,1,0:T(8,128)S(1)} %get-tuple-element.6.done, f32[2,16,128]{2,1,0:T(8,128)S(1)} %get-tuple-element.7.wind_new, bf16[1152,256]{1,0:T(8,128)(2,1)S(1)} %get-tuple-element.8.weights, f32[1,256]{1,0:T(1,128)S(1)} %get-tuple-element.9.mask), custom_call_target="tpu_custom_call" | custom-call | tf_op jit(solution)/shard_map/pallas_call | solution.py:490

commit v4 on v3

--- a/solution.py
+++ b/solution.py
@@ -11,7 +11,6 @@
 CHEM_STEPS = 3
 WIND_STAGES = 3
 PARTS = 2
-PIECES = 2
 FLOW = 6
 LEAD = (2, 1)
 EARLY = 2
@@ -26,7 +25,7 @@
 
 
 def chemistry(weights, concs, masks, store=None):
-    species = concs[0].shape[0]
+    species, width = concs[0].shape
     block = species // PARTS
     height = weights.shape[0] // PARTS
     pairs = (height // block - 1) // 2
@@ -35,14 +34,13 @@
             conc = concs[j]
             high = conc.astype(jnp.bfloat16)
             low = (conc - high.astype(jnp.float32)).astype(jnp.bfloat16)
-            high = jnp.concatenate([high, high], axis=0)
-            low = jnp.concatenate([low, low], axis=0)
+            parts = jnp.concatenate([high, low], axis=1)
+            parts = jnp.concatenate([parts, parts], axis=0)
             blocks = []
             for part in range(PARTS):
                 lhs = weights[part * height : (part + 1) * height]
-                terms = jnp.dot(lhs, high, preferred_element_type=jnp.float32) + jnp.dot(
-                    lhs, low, preferred_element_type=jnp.float32
-                )
+                terms = jnp.dot(lhs, parts, preferred_element_type=jnp.float32)
+                terms = terms[:, :width] + terms[:, width:]
                 rate = terms[:block]
                 for p in range(pairs):
                     one = (1 + p) * block
@@ -50,7 +48,7 @@
                     rate += terms[one : one + block] * terms[two : two + block]
                 blocks.append(conc[part * block : (part + 1) * block] + rate * mask)
                 if store is not None and step == CHEM_STEPS - 1:
-                    store(part, blocks[-1])
+                    store(part, j, blocks[-1])
                 yield
             concs[j] = jnp.concatenate(blocks, axis=0)
 
@@ -295,20 +293,18 @@
     count = count_ref[0]
     lane = lax.broadcasted_iota(jnp.int32, (1, width), 1)
 
-    def mask_of(*pair):
-        cell = jnp.concatenate([(i - depth) * width + lane for i in pair], axis=1)
-        return jnp.where(cell < count, 1.0, 0.0)
+    def mask_of(i):
+        return jnp.where((i - depth) * width + lane < count, 1.0, 0.0)
 
     def react(couples, values=None):
         concs, masks = [], []
         for n, (first, second) in enumerate(couples):
             pair = (lev[depth, first], lev[depth, second]) if values is None else values[n]
-            concs.append(jnp.concatenate(pair, axis=1))
-            masks.append(mask_of(first, second))
+            concs.extend(pair)
+            masks.extend(mask_of(i) for i in (first, second))
         yield from chemistry(weights, concs, masks)
-        for (first, second), conc in zip(couples, concs):
-            done[first - depth] = conc[:, :width]
-            done[second - depth] = conc[:, width:]
+        for i, conc in zip((i for couple in couples for i in couple), concs):
+            done[i - depth] = conc
 
     def weave(main, side=(), pace=1):
         side = iter(side)
@@ -366,7 +362,7 @@
             yield from part
 
     halfway = base + rows // 2
-    pace = -(-2 * depth // (PARTS * CHEM_STEPS))
+    pace = -(-2 * depth // (2 * PARTS * CHEM_STEPS))
 
     def one_side(side):
         wind_send(side).wait_recv()
@@ -408,7 +404,7 @@
     for k in range(depth - 1):
         values = arrive(0, 1, k)
         weave(react([couples[1 + WIND_STAGES + k]], [values]), both_ready(k + 1), pace)
-    mask_out[...] = mask_of(low, high - 1)
+    mask_out[0], mask_out[1] = mask_of(low), mask_of(high - 1)
     done[0], done[rows - 1] = arrive(0, 1, depth - 1)
     for side in range(2):
         wind_send(side).wait_send()
@@ -424,22 +420,17 @@
         copies.append(pltpu.make_async_copy(done.at[r], tracers_out.at[:, r, :], out_sem.at[r]))
     rest = iter(list(copies))
 
-    def store(part, values):
+    def store(part, end, values):
         own = slice(part * block, (part + 1) * block)
-        tail[0, own] = values[:, :width]
-        tail[1, own] = values[:, width:]
-        if (part + 1) % (PARTS // PIECES) == 0:
-            piece = (part + 1) // (PARTS // PIECES) - 1
-            span = slice(piece * species // PIECES, (piece + 1) * species // PIECES)
-            for end, r in ((0, 0), (1, rows - 1)):
-                copy = pltpu.make_async_copy(
-                    tail.at[end, span], tracers_out.at[span, r, :], tail_sem.at[end, piece]
-                )
-                copy.start()
-                copies.append(copy)
-
-    conc = jnp.concatenate([done[0], done[rows - 1]], axis=1)
-    for _ in chemistry(weights, [conc], [mask[...]], store):
+        tail[end, own] = values
+        copy = pltpu.make_async_copy(
+            tail.at[end, own], tracers_out.at[own, end * (rows - 1), :], tail_sem.at[end, part]
+        )
+        copy.start()
+        copies.append(copy)
+
+    ends = [done[0], done[rows - 1]]
+    for _ in chemistry(weights, ends, [mask[0], mask[1]], store):
         for copy in (next(rest, None) for _ in range(FLOW)):
             if copy is not None:
                 copy.start()
@@ -463,7 +454,7 @@
             pltpu.VMEM((rows, species, width), f32),
             pltpu.VMEM(winds.shape, f32),
             pltpu.VMEM((lines, 2 * species), jnp.bfloat16),
-            pltpu.VMEM((1, 2 * width), f32),
+            pltpu.VMEM((2, 1, width), f32),
         ),
         in_specs=[anywhere] * 7,
         out_specs=(vmem,) * 4,
@@ -495,7 +486,7 @@
         ),
         in_specs=[vmem] * 4,
         out_specs=(anywhere, anywhere),
-        scratch_shapes=[pltpu.VMEM((2, species, width), f32), dma((rows,)), dma((2, PIECES)), dma],
+        scratch_shapes=[pltpu.VMEM((2, species, width), f32), dma((rows,)), dma((2, PARTS)), dma],
     )(*(pltpu.with_memory_space_constraint(x, pltpu.VMEM) for x in held_over))
 
 

time: 20.7 us -> 19.8 us (0.957)
  Pallas kernels: 18.9 us -> 18 us
    pallas_call x1, Pallas kernels: 16.6 us -> 16.1 us  [on_device(): pl.pallas_call(functools.partial(kernel, sizes), out_shape=(pltpu.VMEM((r...]
    pallas_call x1, Pallas kernels: 2.27 us -> 1.92 us  [on_device(): pl.pallas_call(finish, out_shape=(jax.ShapeDtypeStruct(tracers.shape, f32...]
where the time goes in v4:
time: 19.8 us; the launch traced here: 19.5 us
  Pallas kernels  18 us (91%)
  between operations  1.45 us (7%)
    pallas_call x1, Pallas kernels, on_device(): pl.pallas_call(functools.partial(kernel, sizes), out_shape=(pltpu.VMEM((r...  16.1 us
    pallas_call x1, Pallas kernels, on_device(): pl.pallas_call(finish, out_shape=(jax.ShapeDtypeStruct(tracers.shape, f32...  1.92 us

profile of v4, /device:TPU:0, one launch (start us, length us, event | category | flops | bytes accessed | tf_op | source)
XLA Modules:
  0.0 19.5 jit_solution(232085980291643051)
XLA Ops:
  1.3 16.1 %shard_map.86 = (f32[16,128,128]{2,1,0:T(8,128)S(1)}, f32[2,16,128]{2,1,0:T(8,128)S(1)}, bf16[1152,256]{1,0:T(8,128)(2,1)S(1)}, f32[2,1,128]{2,1,0:T(1,128)S(1)}) custom-call(s32[1]{0:T(128)S(6)} %copy.9.active, f32[128,16,128]{2,1,0:T(8,128)} %tracers.1, f32[2,16,128]{2,1,0:T(8,128)} %winds.1, f32[128,128]{1,0:T(8,128)} %linear.1, f32[1,128]{1,0:T(1,128)} %bitcast.1, ...), custom_call_target="tpu_custom_call" | custom-call | tf_op jit(solution)/shard_map/pallas_call | solution.py:451
  17.4 1.9 %shard_map.87 = (f32[128,16,128]{2,1,0:T(8,128)}, f32[2,16,128]{2,1,0:T(8,128)}) custom-call(f32[16,128,128]{2,1,0:T(8,128)S(1)} %get-tuple-element.6.done, f32[2,16,128]{2,1,0:T(8,128)S(1)} %get-tuple-element.7.wind_new, bf16[1152,256]{1,0:T(8,128)(2,1)S(1)} %get-tuple-element.8.weights, f32[2,1,128]{2,1,0:T(1,128)S(1)} %get-tuple-element.9.mask), custom_call_target="tpu_custom_call" | custom-call | tf_op jit(solution)/shard_map/pallas_call | solution.py:481

commit v5 on v4

--- a/solution.py
+++ b/solution.py
@@ -191,9 +191,15 @@
 
     @pl.when(jnp.logical_and(place > 0, place < last))
     def _():
-        send(1)
+        wind_send(1).start()
+        for k in range(2):
+            halo_send(1, k).start()
         pl.semaphore_wait(joined, 1)
-        send(0)
+        wind_send(0).start()
+        for k in range(depth):
+            halo_send(0, k).start()
+            if k + 2 < depth:
+                halo_send(1, k + 2).start()
 
     @pl.when(place == last)
     def _():

time: 19.8 us -> 19.8 us (level)
  no operation moved by 1% of the time
where the time goes in v5:
time: 19.8 us; the launch traced here: 19.5 us
  Pallas kernels  18 us (91%)
  between operations  1.45 us (7%)
    pallas_call x1, Pallas kernels, on_device(): pl.pallas_call(functools.partial(kernel, sizes), out_shape=(pltpu.VMEM((r...  16.1 us
    pallas_call x1, Pallas kernels, on_device(): pl.pallas_call(finish, out_shape=(jax.ShapeDtypeStruct(tracers.shape, f32...  1.92 us

profile of v5, /device:TPU:0, one launch (start us, length us, event | category | flops | bytes accessed | tf_op | source)
XLA Modules:
  0.0 19.5 jit_solution(9119995920599453219)
XLA Ops:
  1.3 16.1 %shard_map.86 = (f32[16,128,128]{2,1,0:T(8,128)S(1)}, f32[2,16,128]{2,1,0:T(8,128)S(1)}, bf16[1152,256]{1,0:T(8,128)(2,1)S(1)}, f32[2,1,128]{2,1,0:T(1,128)S(1)}) custom-call(s32[1]{0:T(128)S(6)} %copy.9.active, f32[128,16,128]{2,1,0:T(8,128)} %tracers.1, f32[2,16,128]{2,1,0:T(8,128)} %winds.1, f32[128,128]{1,0:T(8,128)} %linear.1, f32[1,128]{1,0:T(1,128)} %bitcast.1, ...), custom_call_target="tpu_custom_call" | custom-call | tf_op jit(solution)/shard_map/pallas_call | solution.py:457
  17.4 1.9 %shard_map.87 = (f32[128,16,128]{2,1,0:T(8,128)}, f32[2,16,128]{2,1,0:T(8,128)}) custom-call(f32[16,128,128]{2,1,0:T(8,128)S(1)} %get-tuple-element.6.done, f32[2,16,128]{2,1,0:T(8,128)S(1)} %get-tuple-element.7.wind_new, bf16[1152,256]{1,0:T(8,128)(2,1)S(1)} %get-tuple-element.8.weights, f32[2,1,128]{2,1,0:T(1,128)S(1)} %get-tuple-element.9.mask), custom_call_target="tpu_custom_call" | custom-call | tf_op jit(solution)/shard_map/pallas_call | solution.py:487
